TPU v7x, 32 devices: a whole 2x2x4 slice. The times are simulated.
32 devices in a mesh: space: 8 (over z, core), set: 4 (over y, x).
Axes of the slice: x: 2, y: 2, z: 4, core: 2. Of those that a mesh axis runs over, the one named last changes fastest.
Arguments:
- initial: float32 [8, 64, 256, 128], P('set', 'space'), may hold values from -6 to 6
- conductivity: float32 [64, 256, 128], P('space'), may hold values from 0.3 to 1
- weights: float32 [8, 64, 256, 128], P('set', 'space'), may hold values from -6 to 6
- setting_index: int32 [8], P('set'), may hold values from 0 to 63
- track: int32 [64, 4], replicated, may hold values from 0 to 255
- power: int32 [64, 4], replicated, may hold values from 0 to 3
Outputs:
- final_temperature: float32 [8, 64, 256, 128], P('set', 'space')
- conductivity_gradient: float32 [64, 256, 128], P('space', 'set')
All inputs are finite; a program needn't handle non-finite values.
Results may differ from a plain program's by a relative error of at most 0.00002.
Values sent between devices are 32-bit elements; how exact they have to be, the bound alone decides.
No kernel may reach another device: no remote copies, remote signals or barrier semaphores. Data moves between devices by JAX's collectives and lax.ppermute only.
A program may use at most 128 MiB of HBM per device.

v0:
```python
import jax
import jax.numpy as jnp
from jax import lax
from jax.sharding import PartitionSpec as P

STEPS = 4


DT = 0.15


def with_halo(shard, sides, width):
    for axis, dim in sides:
        size, length = (lax.axis_size(axis), shard.shape[dim])
        up = [(i, (i + 1) % size) for i in range(size - 1)]
        down = [(j, i) for i, j in up]
        last = lax.slice_in_dim(shard, length - width, length, axis=dim)
        initial = lax.slice_in_dim(shard, 0, width, axis=dim)
        before = lax.ppermute(last, axis, up)
        after = lax.ppermute(initial, axis, down)
        shard = jnp.concatenate([before, shard, after], axis=dim)
    return shard


def conduct(thermal):
    return 1.0 / (1.0 + thermal * thermal)


def conduct_slope(thermal):
    inverse = 1.0 / (1.0 + thermal * thermal)
    return -2.0 * thermal * inverse * inverse


def pad_cross(values):
    return jnp.pad(values, ((0, 0), (0, 0), (1, 1), (1, 1)))


def neighbours(padded):
    return [
        padded[:, 2:, 1:-1, 1:-1],
        padded[:, :-2, 1:-1, 1:-1],
        padded[:, 1:-1, 2:, 1:-1],
        padded[:, 1:-1, :-2, 1:-1],
        padded[:, 1:-1, 1:-1, 2:],
        padded[:, 1:-1, 1:-1, :-2],
    ]


def local(initial, conductivity, weights, setting_index, track, power):
    y_count = initial.shape[2]
    z_count = initial.shape[3]
    onehot = (
        setting_index[:, None] == jnp.arange(track.shape[0], dtype=jnp.int32)[None, :]
    ).astype(jnp.int32)
    y_track = jnp.sum(onehot[:, :, None] * track[None], axis=1)
    levels = jnp.sum(onehot[:, :, None] * power[None], axis=1)
    y_cells = jnp.arange(y_count).astype(jnp.float32)
    z_cells = jnp.arange(z_count).astype(jnp.float32)
    prof_z = jnp.exp(-4.0 * z_cells / z_count)
    kappa = conductivity[None]
    saved = []
    kappa_ext = with_halo(conductivity, (("space", 0),), 1)
    thermal = initial
    for index_step in range(STEPS):
        temp_ext = with_halo(thermal, (("space", 1),), 1)
        coef_ext = kappa_ext[None] * conduct(temp_ext)
        padded_temp = pad_cross(temp_ext)
        padded_coef = pad_cross(coef_ext)
        saved.append((padded_temp, padded_coef))
        centre_coef = padded_coef[:, 1:-1, 1:-1, 1:-1]
        flux = jnp.zeros_like(thermal)
        for near_temp, near_coef in zip(neighbours(padded_temp), neighbours(padded_coef)):
            flux = flux + 0.5 * (centre_coef + near_coef) * (near_temp - thermal)
        y_start = y_track[:, index_step].astype(jnp.float32)
        power_level = levels[:, index_step].astype(jnp.float32)
        offset = (y_cells[None, :] - y_start[:, None]) * 16.0 / y_count
        prof_y = jnp.exp(-(offset * offset))
        scale = 0.5 * (1.0 + power_level)
        thermal = thermal + DT * (
            flux
            + scale[:, None, None, None] * prof_y[:, None, :, None] * prof_z[None, None, None, :]
        )
    adjoint = weights
    gradient = jnp.zeros(conductivity.shape, jnp.float32)
    for index_step in reversed(range(STEPS)):
        padded_temp, padded_coef = saved[index_step]
        adj_ext = with_halo(adjoint, (("space", 1),), 1)
        padded_adj = pad_cross(adj_ext)
        centre_temp = padded_temp[:, 1:-1, 1:-1, 1:-1]
        centre_coef = padded_coef[:, 1:-1, 1:-1, 1:-1]
        grad_temp = adjoint
        grad_coef = jnp.zeros_like(adjoint)
        for near_temp, near_coef, near_adj in zip(
            neighbours(padded_temp), neighbours(padded_coef), neighbours(padded_adj)
        ):
            grad_temp = grad_temp + DT * 0.5 * (centre_coef + near_coef) * (near_adj - adjoint)
            grad_coef = grad_coef + 0.5 * DT * (near_temp - centre_temp) * (adjoint - near_adj)
        gradient = gradient + jnp.sum(grad_coef * conduct(centre_temp), axis=0)
        adjoint = grad_temp + grad_coef * kappa * conduct_slope(centre_temp)
    owned = lax.psum_scatter(gradient, "set", scatter_dimension=1, tiled=True)
    return (thermal, owned)


def solution(mesh):
    in_specs = (
        P("set", "space", None, None),
        P("space", None, None),
        P("set", "space", None, None),
        P("set"),
        P(),
        P(),
    )
    out_specs = (P("set", "space", None, None), P("space", "set", None))
    return jax.shard_map(local, mesh=mesh, in_specs=in_specs, out_specs=out_specs, check_vma=False)
```

profile of v0, /device:TPU:0, one launch (start us, length us, event | category | flops | bytes accessed | tf_op | source)
XLA Modules:
  0.0 239.3 jit_solution(10804609303899555021)
XLA Ops:
  7.2 1.1 fusion.152
  8.3 2.4 %collective-permute-start = (f32[1,256,128]{2,1,0:T(8,128)S(1)}, f32[1,256,128]{2,1,0:T(8,128)S(1)}, u32[]{:S(2)}, u32[]{:S(2)}) collective-permute-start(f32[1,256,128]{2,1,0:T(8,128)S(1)} %get-tuple-element.40), channel_id=1, source_target_pairs={{0,4},{4,8},{8,12},{12,16},{16,20},{20,24},{24,28},{1,5},{5,9},{9,... | collective-permute-start | bytes 393224 | tf_op jit(solution)/shard_map/ppermute | solution.py:19
  10.7 1.3 collective-permute-start.1
  12.0 1.1 fusion.151
  13.1 1.3 collective-permute-start.3
  14.4 5.8 %collective-permute-start.2 = (f32[2,1,256,128]{3,2,1,0:T(8,128)S(1)}, f32[2,1,256,128]{3,2,1,0:T(8,128)S(1)}, u32[]{:S(2)}, u32[]{:S(2)}) collective-permute-start(f32[2,1,256,128]{3,2,1,0:T(8,128)S(1)} %get-tuple-element.39), channel_id=1, source_target_pairs={{0,4},{4,8},{8,12},{12,16},{16,20},{20,24},{24,28},{1,5},{5,9},{9,... | collective-permute-start | bytes 786440 | tf_op jit(solution)/shard_map/ppermute | solution.py:19
  20.3 0.7 compare_convert_fusion
  21.0 0.8 multiply_reduce_fusion.3
  22.2 1.0 broadcast_multiply_fusion
  24.8 0.9 copy-done.5
  25.8 3.5 %fusion.18 = f32[2,8,256,128]{3,2,1,0:T(8,128)S(1)} fusion(f32[2,8,256,128]{3,2,1,0:T(8,128)S(1)} %copy-done.11, f32[2,10,256,128]{3,2,1,0:T(8,128)S(1)} %divide_multiply_fusion.3, f32[2,10,256,128]{3,2,1,0:T(8,128)S(1)} %constant_dynamic-update-slice_fusion, f32[2,1,256,128]{3,2,1,0:T(8,128)S(1)} %collective-permute-done.3, ...), kind=kLoop, calls=%fused_computation.72 | loop fusion | flops 17825792 | bytes 16515072 | tf_op jit(solution)/shard_map/add | solution.py:79
  29.3 3.6 %collective-permute-start.4 = (f32[2,1,256,128]{3,2,1,0:T(8,128)S(1)}, f32[2,1,256,128]{3,2,1,0:T(8,128)S(1)}, u32[]{:S(2)}, u32[]{:S(2)}) collective-permute-start(f32[2,1,256,128]{3,2,1,0:T(8,128)S(1)} %get-tuple-element.36), channel_id=1, source_target_pairs={{0,4},{4,8},{8,12},{12,16},{16,20},{20,24},{24,28},{1,5},{5,9},{9,... | collective-permute-start | bytes 786440 | tf_op jit(solution)/shard_map/ppermute | solution.py:19
  33.0 1.3 collective-permute-start.5
  34.3 3.7 %collective-permute-done.5 = f32[2,1,256,128]{3,2,1,0:T(8,128)S(1)} collective-permute-done((f32[2,1,256,128]{3,2,1,0:T(8,128)S(1)}, f32[2,1,256,128]{3,2,1,0:T(8,128)S(1)}, u32[]{:S(2)}, u32[]{:S(2)}) %collective-permute-start.5) | collective-permute-done | bytes 262176 | tf_op jit(solution)/shard_map/ppermute | solution.py:20
  38.6 3.5 %multiply_add_fusion.2 = f32[2,8,256,128]{3,2,1,0:T(8,128)S(1)} fusion(f32[2,8,256,128]{3,2,1,0:T(8,128)S(1)} %fusion.18, f32[2,1,256,128]{3,2,1,0:T(8,128)S(1)} %collective-permute-done.5, f32[2,1,256,128]{3,2,1,0:T(8,128)S(1)} %collective-permute-done.4, f32[2,256,128]{2,1,0:T(8,128)S(1)} %get-tuple-element.47, ...), kind=kLoop, calls=%fused_computation.231 | loop fusion | flops 17825792 | bytes 16515072 | tf_op jit(solution)/shard_map/add | solution.py:79
  42.2 6.7 %collective-permute-start.6 = (f32[2,1,256,128]{3,2,1,0:T(8,128)S(1)}, f32[2,1,256,128]{3,2,1,0:T(8,128)S(1)}, u32[]{:S(2)}, u32[]{:S(2)}) collective-permute-start(f32[2,1,256,128]{3,2,1,0:T(8,128)S(1)} %get-tuple-element.34), channel_id=1, source_target_pairs={{0,4},{4,8},{8,12},{12,16},{16,20},{20,24},{24,28},{1,5},{5,9},{9,... | collective-permute-start | bytes 786440 | tf_op jit(solution)/shard_map/ppermute | solution.py:19
  48.9 1.3 collective-permute-start.7
  50.3 1.3 collective-permute-start.10
  51.6 3.7 %collective-permute-start.11 = (f32[2,1,256,128]{3,2,1,0:T(8,128)S(1)}, f32[2,1,256,128]{3,2,1,0:T(8,128)S(1)}, u32[]{:S(2)}, u32[]{:S(2)}) collective-permute-start(f32[2,1,256,128]{3,2,1,0:T(8,128)S(1)} %get-tuple-element.31), channel_id=1, source_target_pairs={{0,4},{4,8},{8,12},{12,16},{16,20},{20,24},{24,28},{1,5},{5,9},{9,... | collective-permute-start | bytes 786440 | tf_op jit(solution)/shard_map/ppermute | solution.py:19
  56.0 3.6 %multiply_add_fusion.1 = f32[2,8,256,128]{3,2,1,0:T(8,128)S(1)} fusion(f32[2,8,256,128]{3,2,1,0:T(8,128)S(1)} %multiply_add_fusion.2, f32[2,1,256,128]{3,2,1,0:T(8,128)S(1)} %collective-permute-done.7, f32[2,1,256,128]{3,2,1,0:T(8,128)S(1)} %collective-permute-done.6, f32[2,256,128]{2,1,0:T(8,128)S(1)} %get-tuple-element.48, ...), kind=kLoop, calls=%fused_computation.230 | loop fusion | flops 17825792 | bytes 16515072 | tf_op jit(solution)/shard_map/add | solution.py:79
  59.7 3.6 %collective-permute-start.8 = (f32[2,1,256,128]{3,2,1,0:T(8,128)S(1)}, f32[2,1,256,128]{3,2,1,0:T(8,128)S(1)}, u32[]{:S(2)}, u32[]{:S(2)}) collective-permute-start(f32[2,1,256,128]{3,2,1,0:T(8,128)S(1)} %get-tuple-element.32), channel_id=1, source_target_pairs={{0,4},{4,8},{8,12},{12,16},{16,20},{20,24},{24,28},{1,5},{5,9},{9,... | collective-permute-start | bytes 786440 | tf_op jit(solution)/shard_map/ppermute | solution.py:19
  63.3 1.5 collective-permute-start.9
  64.9 3.8 %select_maximum_fusion.6 = f32[2,10,258,130]{3,2,1,0:T(8,128)} fusion(f32[2,1,256,128]{3,2,1,0:T(8,128)S(1)} %collective-permute-done.10, f32[2,8,256,128]{3,2,1,0:T(8,128)S(1)} %copy-done.13, f32[2,1,256,128]{3,2,1,0:T(8,128)S(1)} %collective-permute-done.11), kind=kLoop, calls=%fused_computation.42 | loop fusion | flops 10062000 | bytes 5304640 | tf_op jit(solution)/shard_map/concatenate | solution.py:21
  69.4 12.8 %multiply_reduce_fusion.2 = (f32[8,256,128]{2,1,0:T(8,128)}, f32[2,8,256,128]{3,2,1,0:T(8,128)}) fusion(f32[2,8,256,128]{3,2,1,0:T(8,128)S(1)} %multiply_add_fusion.1, f32[2,8,256,128]{3,2,1,0:T(8,128)} %param.8, f32[2,10,258,130]{3,2,1,0:T(8,128)} %select_maximum_fusion.6, f32[2,10,256,128]{3,2,1,0:T(8,128)S(1)} %get-tuple-element.18, ...), kind=kLoop, calls=%fused_computation.227 | loop fusion | flops 19660800 | bytes 19398656 | tf_op jit(solution)/shard_map/reduce_sum | solution.py:98
  82.2 12.6 %fusion.4 = f32[2,8,256,128]{3,2,1,0:T(8,128)} fusion(f32[2,8,256,128]{3,2,1,0:T(8,128)} %param.8, f32[2,1,256,128]{3,2,1,0:T(8,128)} %copy-done.26, f32[2,1,256,128]{3,2,1,0:T(8,128)} %copy-done.25, f32[2,8,256,128]{3,2,1,0:T(8,128)} %copy-done, f32[2,8,256,128]{3,2,1,0:T(8,128)} %get-tuple-element.15, f32[2,10,258,130]{3,2,1,0:T(8,128)} %select_maximum_fusion.6, ...), kind=kLoop, calls=%fused_computation.58 | loop fusion | flops 21495808 | bytes 27262976 | tf_op jit(solution)/shard_map/add | solution.py:99
  94.8 1.1 fusion.146
  95.9 1.3 collective-permute-start.12
  97.2 5.1 %collective-permute-start.13 = (f32[2,1,256,128]{3,2,1,0:T(8,128)S(1)}, f32[2,1,256,128]{3,2,1,0:T(8,128)S(1)}, u32[]{:S(2)}, u32[]{:S(2)}) collective-permute-start(f32[2,1,256,128]{3,2,1,0:T(8,128)S(1)} %get-tuple-element.29), channel_id=1, source_target_pairs={{0,4},{4,8},{8,12},{12,16},{16,20},{20,24},{24,28},{1,5},{5,9},{9,... | collective-permute-start | bytes 786440 | tf_op jit(solution)/shard_map/ppermute | solution.py:19
  102.3 1.1 collective-permute-done.13
  103.5 5.1 %select_maximum_fusion.4 = f32[2,10,258,130]{3,2,1,0:T(8,128)} fusion(f32[2,1,256,128]{3,2,1,0:T(8,128)S(1)} %collective-permute-done.12, f32[2,8,256,128]{3,2,1,0:T(8,128)} %fusion.4, f32[2,1,256,128]{3,2,1,0:T(8,128)S(1)} %collective-permute-done.13), kind=kLoop, calls=%fused_computation.40 | loop fusion | flops 10062000 | bytes 5304640 | tf_op jit(solution)/shard_map/concatenate | solution.py:21
  108.6 14.9 %multiply_reduce_fusion.1 = (f32[8,256,128]{2,1,0:T(8,128)}, f32[2,8,256,128]{3,2,1,0:T(8,128)}) fusion(f32[2,8,256,128]{3,2,1,0:T(8,128)S(1)} %copy-done.2, f32[2,8,256,128]{3,2,1,0:T(8,128)S(1)} %copy-done.4, f32[2,10,258,130]{3,2,1,0:T(8,128)} %select_maximum_fusion.4, f32[2,10,256,128]{3,2,1,0:T(8,128)} %copy-done.10, ...), kind=kLoop, calls=%fused_computation.225 | loop fusion | flops 19660800 | bytes 19398656 | tf_op jit(solution)/shard_map/reduce_sum | solution.py:98
  123.5 12.7 %fusion.6 = f32[2,8,256,128]{3,2,1,0:T(8,128)} fusion(f32[2,8,256,128]{3,2,1,0:T(8,128)} %fusion.4, f32[2,1,256,128]{3,2,1,0:T(8,128)} %copy-done.29, f32[2,1,256,128]{3,2,1,0:T(8,128)} %copy-done.27, f32[2,8,256,128]{3,2,1,0:T(8,128)} %copy-done.1, f32[2,8,256,128]{3,2,1,0:T(8,128)} %get-tuple-element.13, f32[2,10,258,130]{3,2,1,0:T(8,128)} %select_maximum_fusion.4, ...), kind=kLoop, calls=%fused_computation.60 | loop fusion | flops 21495808 | bytes 27262976 | tf_op jit(solution)/shard_map/add | solution.py:99
  136.2 1.1 fusion.145
  137.2 1.3 collective-permute-start.14
  138.6 6.9 %collective-permute-start.15 = (f32[2,1,256,128]{3,2,1,0:T(8,128)S(1)}, f32[2,1,256,128]{3,2,1,0:T(8,128)S(1)}, u32[]{:S(2)}, u32[]{:S(2)}) collective-permute-start(f32[2,1,256,128]{3,2,1,0:T(8,128)S(1)} %get-tuple-element.27), channel_id=1, source_target_pairs={{0,4},{4,8},{8,12},{12,16},{16,20},{20,24},{24,28},{1,5},{5,9},{9,... | collective-permute-start | bytes 786440 | tf_op jit(solution)/shard_map/ppermute | solution.py:19
  145.5 0.9 collective-permute-done.15
  146.4 5.1 %select_maximum_fusion.2 = f32[2,10,258,130]{3,2,1,0:T(8,128)} fusion(f32[2,1,256,128]{3,2,1,0:T(8,128)S(1)} %collective-permute-done.14, f32[2,8,256,128]{3,2,1,0:T(8,128)} %fusion.6, f32[2,1,256,128]{3,2,1,0:T(8,128)S(1)} %collective-permute-done.15), kind=kLoop, calls=%fused_computation.38 | loop fusion | flops 10062000 | bytes 5304640 | tf_op jit(solution)/shard_map/concatenate | solution.py:21
  151.6 11.0 %multiply_reduce_fusion = (f32[8,256,128]{2,1,0:T(8,128)}, f32[2,8,256,128]{3,2,1,0:T(8,128)}) fusion(f32[2,8,256,128]{3,2,1,0:T(8,128)S(1)} %fusion.18, f32[2,8,256,128]{3,2,1,0:T(8,128)S(1)} %copy-done.3, f32[2,10,258,130]{3,2,1,0:T(8,128)} %select_maximum_fusion.2, f32[2,10,256,128]{3,2,1,0:T(8,128)S(1)} %copy-done.8, ...), kind=kLoop, calls=%fused_computation.223 | loop fusion | flops 19660800 | bytes 19398656 | tf_op jit(solution)/shard_map/reduce_sum | solution.py:98
  162.5 9.9 %fusion.8 = f32[2,8,256,128]{3,2,1,0:T(8,128)} fusion(f32[2,8,256,128]{3,2,1,0:T(8,128)S(1)} %copy-done.3, f32[2,1,256,128]{3,2,1,0:T(8,128)} %copy-done.30, f32[2,1,256,128]{3,2,1,0:T(8,128)} %copy-done.28, f32[2,8,256,128]{3,2,1,0:T(8,128)S(1)} %fusion.18, f32[2,8,256,128]{3,2,1,0:T(8,128)} %get-tuple-element.17, ...), kind=kLoop, calls=%fused_computation.62 | loop fusion | flops 21495808 | bytes 27262976 | tf_op jit(solution)/shard_map/add | solution.py:99
  172.4 1.1 fusion.144
  173.5 6.6 %collective-permute-start.17 = (f32[2,1,256,128]{3,2,1,0:T(8,128)S(1)}, f32[2,1,256,128]{3,2,1,0:T(8,128)S(1)}, u32[]{:S(2)}, u32[]{:S(2)}) collective-permute-start(f32[2,1,256,128]{3,2,1,0:T(8,128)S(1)} %get-tuple-element.24), channel_id=1, source_target_pairs={{0,4},{4,8},{8,12},{12,16},{16,20},{20,24},{24,28},{1,5},{5,9},{9,... | collective-permute-start | bytes 786440 | tf_op jit(solution)/shard_map/ppermute | solution.py:19
  180.1 1.6 collective-permute-start.16
  181.7 4.2 %collective-permute-done.16 = f32[2,1,256,128]{3,2,1,0:T(8,128)S(1)} collective-permute-done((f32[2,1,256,128]{3,2,1,0:T(8,128)S(1)}, f32[2,1,256,128]{3,2,1,0:T(8,128)S(1)}, u32[]{:S(2)}, u32[]{:S(2)}) %collective-permute-start.16) | collective-permute-done | bytes 262176 | tf_op jit(solution)/shard_map/ppermute | solution.py:20
  186.6 3.5 %select_maximum_fusion = f32[2,10,258,130]{3,2,1,0:T(8,128)S(1)} fusion(f32[2,1,256,128]{3,2,1,0:T(8,128)S(1)} %collective-permute-done.16, f32[2,8,256,128]{3,2,1,0:T(8,128)} %fusion.8, f32[2,1,256,128]{3,2,1,0:T(8,128)S(1)} %collective-permute-done.17), kind=kLoop, calls=%fused_computation.36 | loop fusion | flops 10062000 | bytes 5304640 | tf_op jit(solution)/shard_map/concatenate | solution.py:21
  190.1 6.3 %fusion.59 = f32[8,256,128]{2,1,0:T(8,128)} fusion(f32[2,8,256,128]{3,2,1,0:T(8,128)S(1)} %copy-done.14, f32[2,10,258,130]{3,2,1,0:T(8,128)S(1)} %select_maximum_fusion, f32[2,1,256,128]{3,2,1,0:T(8,128)S(1)} %collective-permute-done.17, f32[2,1,256,128]{3,2,1,0:T(8,128)} %copy-done.31, f32[2,8,256,128]{3,2,1,0:T(8,128)S(1)} %copy-done.12, ...), kind=kLoop, calls=%fused_computation.114 | loop fusion | flops 19660800 | bytes 17301504 | tf_op jit(solution)/shard_map/reduce_sum | solution.py:98
  196.4 3.4 %add_add_fusion = f32[8,256,128]{2,1,0:T(8,128)} fusion(f32[8,256,128]{2,1,0:T(8,128)} %fusion.59, f32[8,256,128]{2,1,0:T(8,128)} %get-tuple-element.16, f32[8,256,128]{2,1,0:T(8,128)} %get-tuple-element.14, f32[8,256,128]{2,1,0:T(8,128)} %get-tuple-element.12), kind=kLoop, calls=%fused_computation.233 | loop fusion | flops 786432 | bytes 5242880 | tf_op jit(solution)/shard_map/add | solution.py:98
  199.9 10.0 %multiply_add_fusion = f32[2,8,256,128]{3,2,1,0:T(8,128)} fusion(f32[2,8,256,128]{3,2,1,0:T(8,128)} %copy-done, f32[2,1,256,128]{3,2,1,0:T(8,128)S(1)} %copy-done.18, f32[2,1,256,128]{3,2,1,0:T(8,128)S(1)} %collective-permute-done.8, f32[2,256,128]{2,1,0:T(8,128)S(1)} %copy-done.32, f32[2,10,256,128]{3,2,1,0:T(8,128)S(1)} %get-tuple-element.19, ...), kind=kLoop, calls=%fused_computation.229 | loop fusion | flops 17825792 | bytes 16515072 | tf_op jit(solution)/shard_map/add | solution.py:79
  209.8 22.6 %reduce-scatter.2.cloned.1.call-done = f32[8,64,128]{2,1,0:T(8,128)} async-done(((f32[8,256,128]{2,1,0:T(8,128)}), f32[8,64,128]{2,1,0:T(8,128)}) %reduce-scatter.2.cloned.1.call-update) | async-done | bytes 262160 | tf_op jit(solution)/shard_map/reduce_scatter | solution.py:100
  (97 shorter events, 4.8 us)
Async XLA Ops:
  7.2 16.1 %copy-start.15 = (f32[8,256,128]{2,1,0:T(8,128)S(1)}, f32[8,256,128]{2,1,0:T(8,128)}, u32[]{:S(2)}) copy-start(f32[8,256,128]{2,1,0:T(8,128)} %param.7) | copy-start | bytes 3145732
  7.2 225.3 %reduce-scatter.2.cloned.1.call-start = ((), (), s32[]{:S(2)}) async-start(), calls=%async_computation.1 | async-start | bytes 1310720 | tf_op jit(solution)/shard_map/reduce_scatter | solution.py:100
  8.3 15.0 %collective-permute-start = (f32[1,256,128]{2,1,0:T(8,128)S(1)}, f32[1,256,128]{2,1,0:T(8,128)S(1)}, u32[]{:S(2)}, u32[]{:S(2)}) collective-permute-start(f32[1,256,128]{2,1,0:T(8,128)S(1)} %get-tuple-element.40), channel_id=1, source_target_pairs={{0,4},{4,8},{8,12},{12,16},{16,20},{20,24},{24,28},{1,5},{5,9},{9,... | collective-permute-start | bytes 393224 | tf_op jit(solution)/shard_map/ppermute | solution.py:19
  10.7 12.5 %collective-permute-start.1 = (f32[1,256,128]{2,1,0:T(8,128)S(1)}, f32[1,256,128]{2,1,0:T(8,128)S(1)}, u32[]{:S(2)}, u32[]{:S(2)}) collective-permute-start(f32[1,256,128]{2,1,0:T(8,128)S(1)} %get-tuple-element.41), channel_id=1, source_target_pairs={{4,0},{8,4},{12,8},{16,12},{20,16},{24,20},{28,24},{5,1},{9,5},{13... | collective-permute-start | bytes 393224 | tf_op jit(solution)/shard_map/ppermute | solution.py:20
  13.1 11.0 %collective-permute-start.3 = (f32[2,1,256,128]{3,2,1,0:T(8,128)S(1)}, f32[2,1,256,128]{3,2,1,0:T(8,128)S(1)}, u32[]{:S(2)}, u32[]{:S(2)}) collective-permute-start(f32[2,1,256,128]{3,2,1,0:T(8,128)S(1)} %get-tuple-element.38), channel_id=1, source_target_pairs={{4,0},{8,4},{12,8},{16,12},{20,16},{24,20},{28,24},{5,1},{9,5},{13... | collective-permute-start | bytes 786440 | tf_op jit(solution)/shard_map/ppermute | solution.py:20
  14.4 9.0 %collective-permute-start.2 = (f32[2,1,256,128]{3,2,1,0:T(8,128)S(1)}, f32[2,1,256,128]{3,2,1,0:T(8,128)S(1)}, u32[]{:S(2)}, u32[]{:S(2)}) collective-permute-start(f32[2,1,256,128]{3,2,1,0:T(8,128)S(1)} %get-tuple-element.39), channel_id=1, source_target_pairs={{0,4},{4,8},{8,12},{12,16},{16,20},{20,24},{24,28},{1,5},{5,9},{9,... | collective-permute-start | bytes 786440 | tf_op jit(solution)/shard_map/ppermute | solution.py:19
  22.2 1.7 copy-start.11
  23.4 1.1 copy-start.23
  24.2 1.6 copy-start.5
  29.3 5.0 %collective-permute-start.4 = (f32[2,1,256,128]{3,2,1,0:T(8,128)S(1)}, f32[2,1,256,128]{3,2,1,0:T(8,128)S(1)}, u32[]{:S(2)}, u32[]{:S(2)}) collective-permute-start(f32[2,1,256,128]{3,2,1,0:T(8,128)S(1)} %get-tuple-element.36), channel_id=1, source_target_pairs={{0,4},{4,8},{8,12},{12,16},{16,20},{20,24},{24,28},{1,5},{5,9},{9,... | collective-permute-start | bytes 786440 | tf_op jit(solution)/shard_map/ppermute | solution.py:19
  33.0 5.1 %collective-permute-start.5 = (f32[2,1,256,128]{3,2,1,0:T(8,128)S(1)}, f32[2,1,256,128]{3,2,1,0:T(8,128)S(1)}, u32[]{:S(2)}, u32[]{:S(2)}) collective-permute-start(f32[2,1,256,128]{3,2,1,0:T(8,128)S(1)} %get-tuple-element.37), channel_id=1, source_target_pairs={{4,0},{8,4},{12,8},{16,12},{20,16},{24,20},{28,24},{5,1},{9,5},{13... | collective-permute-start | bytes 786440 | tf_op jit(solution)/shard_map/ppermute | solution.py:20
  38.6 3.6 %copy-start.7 = (f32[2,10,256,128]{3,2,1,0:T(8,128)}, f32[2,10,256,128]{3,2,1,0:T(8,128)S(1)}, u32[]{:S(2)}) copy-start(f32[2,10,256,128]{3,2,1,0:T(8,128)S(1)} %get-tuple-element.22) | copy-start | bytes 7864324
  38.6 11.6 %copy-start.13 = (f32[2,8,256,128]{3,2,1,0:T(8,128)S(1)}, f32[2,8,256,128]{3,2,1,0:T(8,128)}, u32[]{:S(2)}) copy-start(f32[2,8,256,128]{3,2,1,0:T(8,128)} %param.8) | copy-start | bytes 6291460
  42.2 13.7 %copy-start.1 = (f32[2,8,256,128]{3,2,1,0:T(8,128)}, f32[2,8,256,128]{3,2,1,0:T(8,128)S(1)}, u32[]{:S(2)}) copy-start(f32[2,8,256,128]{3,2,1,0:T(8,128)S(1)} %multiply_add_fusion.2) | copy-start | bytes 6291460
  42.2 13.0 %collective-permute-start.6 = (f32[2,1,256,128]{3,2,1,0:T(8,128)S(1)}, f32[2,1,256,128]{3,2,1,0:T(8,128)S(1)}, u32[]{:S(2)}, u32[]{:S(2)}) collective-permute-start(f32[2,1,256,128]{3,2,1,0:T(8,128)S(1)} %get-tuple-element.34), channel_id=1, source_target_pairs={{0,4},{4,8},{8,12},{12,16},{16,20},{20,24},{24,28},{1,5},{5,9},{9,... | collective-permute-start | bytes 786440 | tf_op jit(solution)/shard_map/ppermute | solution.py:19
  48.9 6.3 %collective-permute-start.7 = (f32[2,1,256,128]{3,2,1,0:T(8,128)S(1)}, f32[2,1,256,128]{3,2,1,0:T(8,128)S(1)}, u32[]{:S(2)}, u32[]{:S(2)}) collective-permute-start(f32[2,1,256,128]{3,2,1,0:T(8,128)S(1)} %get-tuple-element.35), channel_id=1, source_target_pairs={{4,0},{8,4},{12,8},{16,12},{20,16},{24,20},{28,24},{5,1},{9,5},{13... | collective-permute-start | bytes 786440 | tf_op jit(solution)/shard_map/ppermute | solution.py:20
  50.3 14.6 %collective-permute-start.10 = (f32[2,1,256,128]{3,2,1,0:T(8,128)S(1)}, f32[2,1,256,128]{3,2,1,0:T(8,128)S(1)}, u32[]{:S(2)}, u32[]{:S(2)}) collective-permute-start(f32[2,1,256,128]{3,2,1,0:T(8,128)S(1)} %get-tuple-element.30), channel_id=1, source_target_pairs={{4,0},{8,4},{12,8},{16,12},{20,16},{24,20},{28,24},{5,1},{9,5},{13... | collective-permute-start | bytes 786440 | tf_op jit(solution)/shard_map/ppermute | solution.py:20
  51.6 13.3 %collective-permute-start.11 = (f32[2,1,256,128]{3,2,1,0:T(8,128)S(1)}, f32[2,1,256,128]{3,2,1,0:T(8,128)S(1)}, u32[]{:S(2)}, u32[]{:S(2)}) collective-permute-start(f32[2,1,256,128]{3,2,1,0:T(8,128)S(1)} %get-tuple-element.31), channel_id=1, source_target_pairs={{0,4},{4,8},{8,12},{12,16},{16,20},{20,24},{24,28},{1,5},{5,9},{9,... | collective-permute-start | bytes 786440 | tf_op jit(solution)/shard_map/ppermute | solution.py:19
  55.9 3.7 %copy-start.10 = (f32[2,10,256,128]{3,2,1,0:T(8,128)}, f32[2,10,256,128]{3,2,1,0:T(8,128)S(1)}, u32[]{:S(2)}) copy-start(f32[2,10,256,128]{3,2,1,0:T(8,128)S(1)} %get-tuple-element.20) | copy-start | bytes 7864324
  59.6 9.8 %copy-start = (f32[2,8,256,128]{3,2,1,0:T(8,128)}, f32[2,8,256,128]{3,2,1,0:T(8,128)S(1)}, u32[]{:S(2)}) copy-start(f32[2,8,256,128]{3,2,1,0:T(8,128)S(1)} %multiply_add_fusion.1) | copy-start | bytes 6291460
  59.7 9.0 %collective-permute-start.8 = (f32[2,1,256,128]{3,2,1,0:T(8,128)S(1)}, f32[2,1,256,128]{3,2,1,0:T(8,128)S(1)}, u32[]{:S(2)}, u32[]{:S(2)}) collective-permute-start(f32[2,1,256,128]{3,2,1,0:T(8,128)S(1)} %get-tuple-element.32), channel_id=1, source_target_pairs={{0,4},{4,8},{8,12},{12,16},{16,20},{20,24},{24,28},{1,5},{5,9},{9,... | collective-permute-start | bytes 786440 | tf_op jit(solution)/shard_map/ppermute | solution.py:19
  63.3 5.4 %collective-permute-start.9 = (f32[2,1,256,128]{3,2,1,0:T(8,128)S(1)}, f32[2,1,256,128]{3,2,1,0:T(8,128)S(1)}, u32[]{:S(2)}, u32[]{:S(2)}) collective-permute-start(f32[2,1,256,128]{3,2,1,0:T(8,128)S(1)} %get-tuple-element.33), channel_id=1, source_target_pairs={{4,0},{8,4},{12,8},{16,12},{20,16},{24,20},{28,24},{5,1},{9,5},{13... | collective-permute-start | bytes 786440 | tf_op jit(solution)/shard_map/ppermute | solution.py:20
  64.8 3.9 %copy-start.25 = (f32[2,1,256,128]{3,2,1,0:T(8,128)}, f32[2,1,256,128]{3,2,1,0:T(8,128)S(1)}, u32[]{:S(2)}) copy-start(f32[2,1,256,128]{3,2,1,0:T(8,128)S(1)} %collective-permute-done.10) | copy-start | bytes 786436
  64.8 3.9 %copy-start.26 = (f32[2,1,256,128]{3,2,1,0:T(8,128)}, f32[2,1,256,128]{3,2,1,0:T(8,128)S(1)}, u32[]{:S(2)}) copy-start(f32[2,1,256,128]{3,2,1,0:T(8,128)S(1)} %collective-permute-done.11) | copy-start | bytes 786436
  69.4 12.8 %copy-start.9 = (f32[2,10,256,128]{3,2,1,0:T(8,128)}, f32[2,10,256,128]{3,2,1,0:T(8,128)S(1)}, u32[]{:S(2)}) copy-start(f32[2,10,256,128]{3,2,1,0:T(8,128)S(1)} %get-tuple-element.18) | copy-start | bytes 7864324
  95.9 6.5 %collective-permute-start.12 = (f32[2,1,256,128]{3,2,1,0:T(8,128)S(1)}, f32[2,1,256,128]{3,2,1,0:T(8,128)S(1)}, u32[]{:S(2)}, u32[]{:S(2)}) collective-permute-start(f32[2,1,256,128]{3,2,1,0:T(8,128)S(1)} %get-tuple-element.28), channel_id=1, source_target_pairs={{4,0},{8,4},{12,8},{16,12},{20,16},{24,20},{28,24},{5,1},{9,5},{13... | collective-permute-start | bytes 786440 | tf_op jit(solution)/shard_map/ppermute | solution.py:20
  97.2 11.4 %copy-start.2 = (f32[2,8,256,128]{3,2,1,0:T(8,128)S(1)}, f32[2,8,256,128]{3,2,1,0:T(8,128)}, u32[]{:S(2)}) copy-start(f32[2,8,256,128]{3,2,1,0:T(8,128)} %copy-done.1) | copy-start | bytes 6291460
  97.2 11.4 %copy-start.4 = (f32[2,8,256,128]{3,2,1,0:T(8,128)S(1)}, f32[2,8,256,128]{3,2,1,0:T(8,128)}, u32[]{:S(2)}) copy-start(f32[2,8,256,128]{3,2,1,0:T(8,128)} %fusion.4) | copy-start | bytes 6291460
  97.2 11.4 %copy-start.20 = (f32[2,1,256,128]{3,2,1,0:T(8,128)S(1)}, f32[2,1,256,128]{3,2,1,0:T(8,128)}, u32[]{:S(2)}) copy-start(f32[2,1,256,128]{3,2,1,0:T(8,128)} %copy-done.19) | copy-start | bytes 786436
  97.2 6.3 %collective-permute-start.13 = (f32[2,1,256,128]{3,2,1,0:T(8,128)S(1)}, f32[2,1,256,128]{3,2,1,0:T(8,128)S(1)}, u32[]{:S(2)}, u32[]{:S(2)}) collective-permute-start(f32[2,1,256,128]{3,2,1,0:T(8,128)S(1)} %get-tuple-element.29), channel_id=1, source_target_pairs={{0,4},{4,8},{8,12},{12,16},{16,20},{20,24},{24,28},{1,5},{5,9},{9,... | collective-permute-start | bytes 786440 | tf_op jit(solution)/shard_map/ppermute | solution.py:19
  102.3 6.2 %copy-start.27 = (f32[2,1,256,128]{3,2,1,0:T(8,128)}, f32[2,1,256,128]{3,2,1,0:T(8,128)S(1)}, u32[]{:S(2)}) copy-start(f32[2,1,256,128]{3,2,1,0:T(8,128)S(1)} %collective-permute-done.12) | copy-start | bytes 786436
  103.5 5.1 %copy-start.29 = (f32[2,1,256,128]{3,2,1,0:T(8,128)}, f32[2,1,256,128]{3,2,1,0:T(8,128)S(1)}, u32[]{:S(2)}) copy-start(f32[2,1,256,128]{3,2,1,0:T(8,128)S(1)} %collective-permute-done.13) | copy-start | bytes 786436
  137.2 8.3 %collective-permute-start.14 = (f32[2,1,256,128]{3,2,1,0:T(8,128)S(1)}, f32[2,1,256,128]{3,2,1,0:T(8,128)S(1)}, u32[]{:S(2)}, u32[]{:S(2)}) collective-permute-start(f32[2,1,256,128]{3,2,1,0:T(8,128)S(1)} %get-tuple-element.26), channel_id=1, source_target_pairs={{4,0},{8,4},{12,8},{16,12},{20,16},{24,20},{28,24},{5,1},{9,5},{13... | collective-permute-start | bytes 786440 | tf_op jit(solution)/shard_map/ppermute | solution.py:20
  138.5 13.0 %copy-start.3 = (f32[2,8,256,128]{3,2,1,0:T(8,128)S(1)}, f32[2,8,256,128]{3,2,1,0:T(8,128)}, u32[]{:S(2)}) copy-start(f32[2,8,256,128]{3,2,1,0:T(8,128)} %fusion.6) | copy-start | bytes 6291460
  138.6 13.0 %copy-start.8 = (f32[2,10,256,128]{3,2,1,0:T(8,128)S(1)}, f32[2,10,256,128]{3,2,1,0:T(8,128)}, u32[]{:S(2)}) copy-start(f32[2,10,256,128]{3,2,1,0:T(8,128)} %copy-done.7) | copy-start | bytes 7864324
  138.6 7.8 %collective-permute-start.15 = (f32[2,1,256,128]{3,2,1,0:T(8,128)S(1)}, f32[2,1,256,128]{3,2,1,0:T(8,128)S(1)}, u32[]{:S(2)}, u32[]{:S(2)}) collective-permute-start(f32[2,1,256,128]{3,2,1,0:T(8,128)S(1)} %get-tuple-element.27), channel_id=1, source_target_pairs={{0,4},{4,8},{8,12},{12,16},{16,20},{20,24},{24,28},{1,5},{5,9},{9,... | collective-permute-start | bytes 786440 | tf_op jit(solution)/shard_map/ppermute | solution.py:19
  145.5 6.0 %copy-start.28 = (f32[2,1,256,128]{3,2,1,0:T(8,128)}, f32[2,1,256,128]{3,2,1,0:T(8,128)S(1)}, u32[]{:S(2)}) copy-start(f32[2,1,256,128]{3,2,1,0:T(8,128)S(1)} %collective-permute-done.14) | copy-start | bytes 786436
  146.4 5.1 %copy-start.30 = (f32[2,1,256,128]{3,2,1,0:T(8,128)}, f32[2,1,256,128]{3,2,1,0:T(8,128)S(1)}, u32[]{:S(2)}) copy-start(f32[2,1,256,128]{3,2,1,0:T(8,128)S(1)} %collective-permute-done.15) | copy-start | bytes 786436
  151.5 11.0 %copy-start.16 = (f32[8,256,128]{2,1,0:T(8,128)S(1)}, f32[8,256,128]{2,1,0:T(8,128)}, u32[]{:S(2)}) copy-start(f32[8,256,128]{2,1,0:T(8,128)} %param.7) | copy-start | bytes 3145732
  173.5 8.2 %collective-permute-start.17 = (f32[2,1,256,128]{3,2,1,0:T(8,128)S(1)}, f32[2,1,256,128]{3,2,1,0:T(8,128)S(1)}, u32[]{:S(2)}, u32[]{:S(2)}) collective-permute-start(f32[2,1,256,128]{3,2,1,0:T(8,128)S(1)} %get-tuple-element.24), channel_id=1, source_target_pairs={{0,4},{4,8},{8,12},{12,16},{16,20},{20,24},{24,28},{1,5},{5,9},{9,... | collective-permute-start | bytes 786440 | tf_op jit(solution)/shard_map/ppermute | solution.py:19
  180.0 10.0 %copy-start.6 = (f32[2,10,256,128]{3,2,1,0:T(8,128)S(1)}, f32[2,10,256,128]{3,2,1,0:T(8,128)}, u32[]{:S(2)}) copy-start(f32[2,10,256,128]{3,2,1,0:T(8,128)} %copy-done.5) | copy-start | bytes 7864324
  180.0 10.0 %copy-start.12 = (f32[2,8,256,128]{3,2,1,0:T(8,128)S(1)}, f32[2,8,256,128]{3,2,1,0:T(8,128)}, u32[]{:S(2)}) copy-start(f32[2,8,256,128]{3,2,1,0:T(8,128)} %param.6) | copy-start | bytes 6291460
  180.1 10.0 %copy-start.14 = (f32[2,8,256,128]{3,2,1,0:T(8,128)S(1)}, f32[2,8,256,128]{3,2,1,0:T(8,128)}, u32[]{:S(2)}) copy-start(f32[2,8,256,128]{3,2,1,0:T(8,128)} %fusion.8) | copy-start | bytes 6291460
  180.1 10.0 %copy-start.22 = (f32[2,1,256,128]{3,2,1,0:T(8,128)S(1)}, f32[2,1,256,128]{3,2,1,0:T(8,128)}, u32[]{:S(2)}) copy-start(f32[2,1,256,128]{3,2,1,0:T(8,128)} %copy-done.21) | copy-start | bytes 786436
  180.1 10.0 %copy-start.24 = (f32[2,1,256,128]{3,2,1,0:T(8,128)S(1)}, f32[2,1,256,128]{3,2,1,0:T(8,128)}, u32[]{:S(2)}) copy-start(f32[2,1,256,128]{3,2,1,0:T(8,128)} %copy-done.23) | copy-start | bytes 786436
  180.1 5.8 %collective-permute-start.16 = (f32[2,1,256,128]{3,2,1,0:T(8,128)S(1)}, f32[2,1,256,128]{3,2,1,0:T(8,128)S(1)}, u32[]{:S(2)}, u32[]{:S(2)}) collective-permute-start(f32[2,1,256,128]{3,2,1,0:T(8,128)S(1)} %get-tuple-element.25), channel_id=1, source_target_pairs={{4,0},{8,4},{12,8},{16,12},{20,16},{24,20},{28,24},{5,1},{9,5},{13... | collective-permute-start | bytes 786440 | tf_op jit(solution)/shard_map/ppermute | solution.py:20
  196.4 3.4 %copy-start.18 = (f32[2,1,256,128]{3,2,1,0:T(8,128)S(1)}, f32[2,1,256,128]{3,2,1,0:T(8,128)}, u32[]{:S(2)}) copy-start(f32[2,1,256,128]{3,2,1,0:T(8,128)} %copy-done.17) | copy-start | bytes 786436
  196.4 3.4 %copy-start.32 = (f32[2,256,128]{2,1,0:T(8,128)S(1)}, f32[2,256,128]{2,1,0:T(8,128)}, u32[]{:S(2)}) copy-start(f32[2,256,128]{2,1,0:T(8,128)} %get-tuple-element.46) | copy-start | bytes 786436
  (4 other events, 2.8 us)
Sparse Core Ops, SparseCore 0:
  200.0 32.4 reduce-scatter.1
where the time goes:
time: 240 us; the launch traced here: 239 us
  other arithmetic  127 us (53%)
  starting transfers between devices  56.6 us (24%)
  waiting for transfers between devices  32.6 us (14%)
  between operations  14.8 us (6%)
  local copies, waits for them, and re-layouts  8.36 us (3%)
    reduce_sum x4, other arithmetic, local(): gradient = gradient + jnp.sum(grad_coef * conduct(centre_temp), axis=0)  44.9 us
    ppermute x9, starting transfers between devices, with_halo(): before = lax.ppermute(last, axis, up)  44.5 us
    add x3, other arithmetic, local(): adjoint = grad_temp + grad_coef * kappa * conduct_slope(centre_temp)  35.1 us
    reduce_scatter x1, waiting for transfers between devices, local(): owned = lax.psum_scatter(gradient, 'set', scatter_dimension=1, tiled=True)  22.6 us
    add x4, other arithmetic, local(): thermal + DT * (flux + scale[:, None, None, None] * prof_y[:, None, :, No...  20.6 us
    concatenate x8, other arithmetic, with_halo(): shard = jnp.concatenate([before, shard, after], axis=dim)  19.5 us
    ppermute x9, starting transfers between devices, with_halo(): after = lax.ppermute(initial, axis, down)  12.1 us
    ppermute x9, waiting for transfers between devices, with_halo(): after = lax.ppermute(initial, axis, down)  7.99 us
  transfers between devices with their start and end apart: 19, of which 5 were waited for; matrix products, arithmetic and copies ran while one was open for 9% of the time, Pallas kernels for 0%

commit v1 on v0

v1 whole, which is shorter than its diff:
```python
import jax
import jax.numpy as jnp
from jax import lax
from jax.experimental import pallas as pl
from jax.experimental.pallas import tpu as pltpu
from jax.sharding import PartitionSpec as P

STEPS = 4
DT = 0.15
HALF = 0.5 * DT
DEPTH = 5
WDEPTH = 2
AHEAD = 14
F32 = jnp.float32


class Geometry:
    def __init__(self, shape):
        self.sets, self.planes, self.rows, self.lanes = shape
        self.tiles = self.rows // 8

    def padded(self, halo):
        return (self.sets, self.planes + 2 * halo, self.tiles + 2, 8, self.lanes)

    def single(self, halo):
        return (self.planes + 2 * halo, self.tiles, 8, self.lanes)

    def tile_row(self, t):
        return pl.ds(t, 8, stride=self.tiles)


def reciprocal(x):
    r = pltpu.reciprocal(x, approx=True)
    return r * (2.0 - x * r)


def loop(lo, hi, body):
    def step(i, _):
        body(i)
        return 0

    lax.fori_loop(lo, hi, step, 0)


class Lanes:
    def __init__(self, geo):
        self.count = geo.lanes
        lane = lax.broadcasted_iota(jnp.int32, (8, geo.lanes), 1)
        sub = lax.broadcasted_iota(jnp.int32, (8, geo.lanes), 0)
        self.inner = jnp.where(lane == geo.lanes - 1, 0.0, 1.0)
        self.ends = jnp.where((lane == geo.lanes - 1) | (lane == 0), 1.0, 0.0)
        self.first, self.last = sub == 0, sub == 7

    def next(self, x):
        return pltpu.roll(x, self.count - 1, 1)

    def previous(self, x):
        return pltpu.roll(x, 1, 1)

    def before(self, tile):
        return jnp.where(self.first, 0.0, pltpu.roll(tile, 1, 0))

    def after(self, tile):
        return jnp.where(self.last, 0.0, pltpu.roll(tile, 7, 0))

    def put(self, ref, s, d, t, tiles, value):
        ref[s, d, t + 1] = value
        if t == 0:
            ref[s, d, tiles + 1] = self.after(value)
        if t == tiles - 1:
            ref[s, d, 0] = self.before(value)


def staged(count, first, second, third):
    one, two = {}, {}
    for i in range(count + 2 * AHEAD):
        if i < count:
            one[i] = first(i)
        j = i - AHEAD
        if 0 <= j < count:
            two[j] = second(j, one.pop(j))
        j = i - 2 * AHEAD
        if 0 <= j < count:
            third(j, two.pop(j))


def weight_of(i, lo, edge):
    return HALF if edge is None else jnp.where(i < -lo, edge, HALF)


def forward(geo, off, lo, hi, u, a, heat, flux, edge, k, k_off, u_next, a_next, out=None):
    lanes = Lanes(geo)
    tiles = geo.tiles

    def start(t):
        for s in range(geo.sets):
            flux[0, s, t] = (a[s, lo + off, t + 1] + a[s, lo - 1 + off, t + 1]) * (
                u[s, lo + off, t + 1] - u[s, lo - 1 + off, t + 1]
            )

    lax.fori_loop(0, tiles, lambda t, c: (start(t), c)[1], 0, unroll=8)

    def plane(i):
        p = i + (lo + off)
        w = weight_of(i, lo, edge)
        items = [(s, t) for s in range(geo.sets) for t in range(tiles)]
        face = {}

        def first(m):
            s, t = items[m]
            return lanes.next(u[s, p, t + 1]), lanes.next(a[s, p, t + 1])

        def second(m, rolled):
            s, t = items[m]
            ur, ar = rolled
            f = (ar + a[s, p, t + 1]) * (ur - u[s, p, t + 1]) * lanes.inner
            return f, lanes.previous(f)

        def third(m, z):
            s, t = items[m]
            uc, ac = u[s, p, t + 1], a[s, p, t + 1]
            if t == 0:
                face[s] = (ac + a[s, p, 0]) * (uc - u[s, p, 0])
            fy = (a[s, p, t + 2] + ac) * (u[s, p, t + 2] - uc)
            fx = (a[s, p + 1, t + 1] + ac) * (u[s, p + 1, t + 1] - uc)
            total = (fx - flux[0, s, t]) + (fy - face[s]) + (z[0] - z[1]) - (ac * uc) * lanes.ends
            face[s] = fy
            flux[0, s, t] = fx
            new = uc + w * (total + heat[s, t])
            if out is not None:
                out(s, i + lo, t, new)
            else:
                lanes.put(u_next, s, p - 1, t, tiles, new)
                lanes.put(a_next, s, p - 1, t, tiles, k[i + (lo + k_off), t] * reciprocal(1.0 + new * new))

        staged(len(items), first, second, third)

    loop(0, hi - lo, plane)


def backward(geo, off, lo, hi, u, a, rk, lam, lam_off, lam_next, next_off, grad, flux, edge):
    lanes = Lanes(geo)
    tiles = geo.tiles
    last = lam_next is None

    def start(t):
        for s in range(geo.sets):
            dl = lam[s, lo + lam_off, t + 1] - lam[s, lo - 1 + lam_off, t + 1]
            flux[0, s, t] = (u[s, lo + off, t + 1] - u[s, lo - 1 + off, t + 1]) * dl
            if not last:
                flux[1, s, t] = (a[s, lo + off, t + 1] + a[s, lo - 1 + off, t + 1]) * dl

    lax.fori_loop(0, tiles, lambda t, c: (start(t), c)[1], 0, unroll=8)

    def plane(i):
        p, q, r = i + (lo + off), i + (lo + lam_off), i + (lo + 1)
        w = weight_of(i, lo, edge)
        items = [(s, t) for t in range(tiles) for s in range(geo.sets)]
        face, parts = {}, {}

        def first(m):
            s, t = items[m]
            rolled = lanes.next(u[s, p, t + 1]), lanes.next(lam[s, q, t + 1])
            return rolled if last else rolled + (lanes.next(a[s, p, t + 1]),)

        def second(m, rolled):
            s, t = items[m]
            dl = (rolled[1] - lam[s, q, t + 1]) * lanes.inner
            e = (rolled[0] - u[s, p, t + 1]) * dl
            if last:
                return e, lanes.previous(e)
            g = (rolled[2] + a[s, p, t + 1]) * dl
            return e, lanes.previous(e), g, lanes.previous(g)

        def third(m, z):
            s, t = items[m]
            uc, ac, lc = u[s, p, t + 1], a[s, p, t + 1], lam[s, q, t + 1]
            if t == 0:
                dl = lc - lam[s, q, 0]
                face[s] = (uc - u[s, p, 0]) * dl, (ac + a[s, p, 0]) * dl
            dl = lam[s, q, t + 2] - lc
            ey, gy = (u[s, p, t + 2] - uc) * dl, (a[s, p, t + 2] + ac) * dl
            dl = lam[s, q + 1, t + 1] - lc
            ex, gx = (u[s, p + 1, t + 1] - uc) * dl, (a[s, p + 1, t + 1] + ac) * dl
            le = lc * lanes.ends
            e = (ex + flux[0, s, t]) + (ey + face[s][0]) + (z[0] + z[1]) + uc * le
            flux[0, s, t] = ex
            b = e * (ac * rk[r, t])
            parts[t] = parts[t] + b if s else b
            if s == geo.sets - 1:
                grad[r, t] += parts.pop(t)
            if not last:
                g = (gx - flux[1, s, t]) + (gy - face[s][1]) + (z[2] - z[3]) - ac * le
                flux[1, s, t] = gx
                b = b * (ac * uc)
                lanes.put(lam_next, s, i + (lo + next_off), t, tiles, lc + w * (g + (b + b)))
            face[s] = ey, gy

        staged(len(items), first, second, third)

    loop(0, hi - lo, plane)


def place():
    me = lax.axis_index("space")
    joined = jnp.where((me == 0) | (me == lax.axis_size("space") - 1), 0, 1)
    return lax.rem(me, 2), joined


def flipped(geo, odd, d):
    return jnp.where(odd == 1, geo.planes - 1 - d, d)


def cut_kernel(geo, refs):
    initial, cond, weights, uo, ko, wo, ui, ki, wi, sems = refs
    odd, _ = place()
    copies = []
    for outer, u, k, w in ((True, uo, ko, wo), (False, ui, ki, wi)):
        def begin(depth):
            return jnp.where((odd == 1) == outer, geo.planes - depth, 0)

        for src, dst in (
            (initial.at[:, pl.ds(begin(DEPTH), DEPTH)], u),
            (cond.at[pl.ds(begin(DEPTH), DEPTH)], k),
            (weights.at[:, pl.ds(begin(WDEPTH), WDEPTH)], w),
        ):
            copies.append(pltpu.make_async_copy(src, dst, sems.at[len(copies)]))
    for c in copies:
        c.start()
    for c in copies:
        c.wait()


STATE = ("u0", "a0", "u1", "a1", "u2", "a2", "u3", "a3", "k", "rk", "lam", "grad", "heat")


def state_shapes(geo):
    shapes = []
    for n in range(STEPS):
        shapes += [geo.padded(DEPTH - n)] * 2
    shapes += [geo.single(DEPTH), geo.single(1), geo.padded(WDEPTH), geo.single(1)]
    return shapes + [(STEPS, geo.sets, geo.tiles, 8, geo.lanes)]


def unpack_plane(geo, lanes, p, value, cond, u0, a0, k):
    for t in range(geo.tiles):
        kap = cond(t)
        k[p, t] = kap
        for s in range(geo.sets):
            val = value(s, t)
            lanes.put(u0, s, p, t, geo.tiles, val)
            lanes.put(a0, s, p, t, geo.tiles, kap * reciprocal(1.0 + val * val))


def first_kernel(geo, refs):
    (initial, cond, weights, index_ref, track_ref, power_ref, u0, a0, u1, a1, u2, a2, u3, a3, k, rk, l4, grad, heat) = refs[:19]
    raw_u, raw_k, raw_w, flux, sems = refs[19:]
    odd, _ = place()
    top = geo.planes
    lanes = Lanes(geo)

    def copies(d):
        p = flipped(geo, odd, d)
        return (
            pltpu.make_async_copy(initial.at[:, p], raw_u.at[:, d], sems.at[0, d]),
            pltpu.make_async_copy(cond.at[p], raw_k.at[d], sems.at[1, d]),
            pltpu.make_async_copy(weights.at[:, p], raw_w.at[:, d], sems.at[2, d]),
        )

    def begin(d):
        for c in copies(d):
            c.start()

    loop(0, top, begin)
    z = lax.broadcasted_iota(jnp.int32, (8, geo.lanes), 1).astype(F32)
    prof_z = jnp.exp(-4.0 * z / geo.lanes)
    sub = lax.broadcasted_iota(jnp.int32, (8, geo.lanes), 0) * geo.tiles

    def warm(i):
        n, s = i // geo.sets, lax.rem(i, geo.sets)
        row = index_ref[s]
        y0 = track_ref[row, n]
        amp = (1.0 + power_ref[row, n].astype(F32)) * prof_z
        for t in range(geo.tiles):
            offset = (sub + (t - y0)).astype(F32) * (16.0 / geo.rows)
            heat[n, s, t] = amp * jnp.exp(-(offset * offset))

    loop(0, STEPS * geo.sets, warm)

    def clear(d):
        grad[d] = jnp.zeros((geo.tiles, 8, geo.lanes), F32)

    loop(0, top + 2, clear)

    def load(d):
        for c in copies(d):
            c.wait()
        unpack_plane(
            geo, lanes, d + DEPTH, lambda s, t: raw_u[s, d, geo.tile_row(t), :], lambda t: raw_k[d, geo.tile_row(t), :], u0, a0, k
        )
        for t in range(geo.tiles):
            rk[d + 1, t] = reciprocal(k[d + DEPTH, t])
            for s in range(geo.sets):
                lanes.put(l4, s, d + WDEPTH, t, geo.tiles, raw_w[s, d, geo.tile_row(t), :])

    loop(0, top, load)
    us, as_ = (u0, u1, u2, u3), (a0, a1, a2, a3)
    for n in range(STEPS - 1):
        forward(
            geo, DEPTH - n, n + 1, top - n - 1, us[n], as_[n], heat.at[n], flux, None, k, DEPTH, us[n + 1], as_[n + 1]
        )


def unpack_halo(geo, odd, u_src, k_src, w_src, u0, a0, k, rk, lam, outer):
    lanes = Lanes(geo)

    def local(j, depth):
        if outer:
            return jnp.where(odd == 1, depth - 1 - j, j)
        return jnp.where(odd == 1, depth - 1 - j, j) + (geo.planes + depth)

    def planes(j):
        unpack_plane(
            geo, lanes, local(j, DEPTH), lambda s, t: u_src[s, j, geo.tile_row(t), :],
            lambda t: k_src[j, geo.tile_row(t), :], u0, a0, k,
        )

    loop(0, DEPTH, planes)

    def more(j):
        for s in range(geo.sets):
            for t in range(geo.tiles):
                lanes.put(lam, s, local(j, WDEPTH), t, geo.tiles, w_src[s, j, geo.tile_row(t), :])

    loop(0, WDEPTH, more)
    d = -1 if outer else geo.planes
    for t in range(geo.tiles):
        rk[d + 1, t] = reciprocal(k[d + DEPTH, t])


def second_kernel(geo, refs):
    (ui, ki, wi) = refs[:3]
    (u0, a0, u1, a1, u2, a2, u3, a3, k, rk, lam, grad, heat, l3, send) = refs[16:31]
    flux = refs[31]
    odd, _ = place()
    top = geo.planes
    unpack_halo(geo, odd, ui, ki, wi, u0, a0, k, rk, lam, False)
    us, as_ = (u0, u1, u2, u3), (a0, a1, a2, a3)
    for n in range(STEPS - 1):
        forward(
            geo, DEPTH - n, top - n - 1, top + DEPTH - 1 - n, us[n], as_[n], heat.at[n], flux, None, k, DEPTH,
            us[n + 1], as_[n + 1],
        )
    backward(geo, 2, top - 4, top + 1, u3, a3, rk, lam, WDEPTH, l3, 1, grad, flux, None)
    backward(geo, 3, top - 3, top, u2, a2, rk, l3, 1, lam, WDEPTH, grad, flux, None)
    for s in range(geo.sets):
        for j in range(WDEPTH):
            send[s, j] = lam[s, top - 1 - j + WDEPTH]


def third_kernel(geo, refs):
    (uo, ko, wo) = refs[:3]
    (u0, a0, u1, a1, u2, a2, u3, a3, k, rk, lam, grad, l3, send) = refs[17:31]
    heat = refs[15]
    flux = refs[31]
    odd, joined = place()
    edge = HALF * joined.astype(F32)

    @pl.when(joined == 0)
    def _():
        zero = jnp.zeros((geo.tiles + 2, 8, geo.lanes), F32)
        def body(j):
            k[j] = zero[: geo.tiles]
            for s in range(geo.sets):
                u0[s, j] = zero
                a0[s, j] = zero

        loop(0, DEPTH, body)
        for s in range(geo.sets):
            for j in range(WDEPTH):
                lam[s, j] = zero
        rk[0] = zero[: geo.tiles]

    @pl.when(joined == 1)
    def _():
        unpack_halo(geo, odd, uo, ko, wo, u0, a0, k, rk, lam, True)

    us, as_ = (u0, u1, u2, u3), (a0, a1, a2, a3)
    for n in range(STEPS - 1):
        forward(
            geo, DEPTH - n, n + 1 - DEPTH, n + 1, us[n], as_[n], heat.at[n], flux, edge, k, DEPTH, us[n + 1], as_[n + 1]
        )
    backward(geo, 2, -1, 3, u3, a3, rk, lam, WDEPTH, l3, 1, grad, flux, edge)
    backward(geo, 3, 0, 2, u2, a2, rk, l3, 1, lam, WDEPTH, grad, flux, edge)
    for s in range(geo.sets):
        for j in range(WDEPTH):
            send[s, j] = lam[s, j + WDEPTH]


def fourth_kernel(geo, refs):
    (u0, a0, u1, a1, u2, a2, u3, a3, rk, heat, received) = refs[:11]
    (final, lam, l3, grad) = refs[14:18]
    flux, raw, sems = refs[18:]
    odd, _ = place()
    top = geo.planes

    def put(s, d, t, value):
        raw[s, d, geo.tile_row(t), :] = value

    forward(geo, 2, 0, top, u3, a3, heat.at[3], flux, None, None, 0, None, None, out=put)

    def copy(d):
        return pltpu.make_async_copy(raw.at[:, d], final.at[:, flipped(geo, odd, d)], sems.at[d])

    loop(0, top, lambda d: copy(d).start())
    for s in range(geo.sets):
        for j in range(WDEPTH):
            lam[s, top + WDEPTH + j] = received[s, j]
    backward(geo, 2, 3, top - 4, u3, a3, rk, lam, WDEPTH, l3, 1, grad, flux, None)
    backward(geo, 3, 2, top - 3, u2, a2, rk, l3, 1, lam, WDEPTH, grad, flux, None)
    backward(geo, 4, 1, top + 1, u1, a1, rk, lam, WDEPTH, l3, 1, grad, flux, None)
    backward(geo, 5, 2, top, u0, a0, rk, l3, 1, None, 0, grad, flux, None)
    loop(0, top, lambda d: copy(d).wait())


def fifth_kernel(geo, ways, refs):
    (u0, a0, u1, a1, rk, received) = refs[:6]
    (lam, l3, grad) = refs[9:12]
    outs = refs[12 : 12 + ways]
    flux, flat = refs[12 + ways :]
    _, joined = place()
    edge = HALF * joined.astype(F32)
    for s in range(geo.sets):
        for j in range(WDEPTH):
            lam[s, WDEPTH - 1 - j] = jnp.where(joined == 1, received[s, j], 0.0)
    backward(geo, 4, -1, 1, u1, a1, rk, lam, WDEPTH, l3, 1, grad, flux, edge)
    backward(geo, 5, 0, 2, u0, a0, rk, l3, 1, None, 0, grad, flux, None)
    me = lax.axis_index("set")
    part = geo.rows // ways

    def spread(d):
        for t in range(geo.tiles):
            flat[geo.tile_row(t), :] = grad[d + 1, t] * (-HALF)
        for way in range(ways):
            outs[way][d] = flat[pl.ds(pl.multiple_of((me ^ way) * part, part), part), :]

    loop(0, geo.planes, spread)


def sum_kernel(geo, refs):
    odd, _ = place()

    def body(d):
        total = refs[0][d]
        for ref in refs[1:-1]:
            total += ref[d]
        refs[-1][flipped(geo, odd, d)] = total

    loop(0, geo.planes, body)


VMEM = pl.BlockSpec(memory_space=pltpu.VMEM)
SMEM = pl.BlockSpec(memory_space=pltpu.SMEM)
HBM = pl.BlockSpec(memory_space=pltpu.HBM)


def pinned(shape):
    return pltpu.VMEM(shape, F32)


def plain(shape):
    return jax.ShapeDtypeStruct(shape, F32)


def call(body, name, ins, in_specs, outs, out_specs=None, aliases=None, scratch=(), mib=4):
    return pl.pallas_call(
        lambda *refs: body(refs),
        name=name,
        out_shape=tuple(outs),
        in_specs=list(in_specs),
        out_specs=tuple(out_specs or [VMEM] * len(outs)),
        scratch_shapes=list(scratch),
        input_output_aliases=aliases or {},
        compiler_params=pltpu.CompilerParams(vmem_limit_bytes=mib * 1024 * 1024),
    )(*ins)


def keep(x):
    return pltpu.with_memory_space_constraint(x, pltpu.VMEM)


def outside(x):
    return pltpu.with_memory_space_constraint(x, pltpu.HBM)


def local(initial, conductivity, weights, setting_index, track, power):
    geo = Geometry(initial.shape)
    top = geo.planes
    spaces, ways = lax.axis_size("space"), lax.axis_size("set")

    both = ("space", "set")
    pairs = [(i, i + 1) for i in range(1, spaces - 1, 2)]
    outer = [(a * ways + c, b * ways + c) for i, j in pairs for a, b in ((i, j), (j, i)) for c in range(ways)]
    outer += [(e * ways + c, e * ways + (c ^ 1)) for e in (0, spaces - 1) for c in range(ways)]
    inner = [(i, i ^ 1) for i in range(spaces)]

    cut_u = (geo.sets, DEPTH, geo.rows, geo.lanes)
    cut_k = (DEPTH, geo.rows, geo.lanes)
    cut_w = (geo.sets, WDEPTH, geo.rows, geo.lanes)
    cuts = call(
        lambda refs: cut_kernel(geo, refs), "cut", tuple(outside(x) for x in (initial, conductivity, weights)), [HBM] * 3,
        [pinned(x) for x in (cut_u, cut_k, cut_w) * 2], scratch=[pltpu.SemaphoreType.DMA((6,))], mib=6,
    )
    uo, ko, wo = (lax.ppermute(x, both, outer) for x in cuts[:3])
    ui, ki, wi = (lax.ppermute(x, "space", inner) for x in cuts[3:])

    flux = pltpu.VMEM((2, geo.sets, geo.tiles, 8, geo.lanes), F32)
    states = [pinned(x) for x in state_shapes(geo)]
    state = call(
        lambda refs: first_kernel(geo, refs), "first",
        tuple(outside(x) for x in (initial, conductivity, weights)) + (setting_index, track, power),
        [HBM] * 3 + [SMEM] * 3, states,
        scratch=[
            pltpu.VMEM(initial.shape, F32), pltpu.VMEM(conductivity.shape, F32), pltpu.VMEM(weights.shape, F32),
            flux, pltpu.SemaphoreType.DMA((3, top)),
        ],
        mib=8,
    )
    l3_shape = pinned(geo.padded(1))
    send = pinned((geo.sets, WDEPTH, geo.tiles + 2, 8, geo.lanes))
    result = call(
        lambda refs: second_kernel(geo, refs), "second",
        tuple(keep(x) for x in (ui, ki, wi) + tuple(state)), [VMEM] * 16, states + [l3_shape, send],
        aliases={3 + i: i for i in range(13)}, scratch=[flux],
    )
    state, l3, send_i = result[:12], result[13], result[14]
    heat = result[12]
    from_inner = lax.ppermute(send_i, "space", inner)
    result = call(
        lambda refs: third_kernel(geo, refs), "third",
        tuple(keep(x) for x in (uo, ko, wo) + tuple(state) + (heat, l3)), [VMEM] * 17, states[:12] + [l3_shape, send],
        aliases={**{3 + i: i for i in range(12)}, 16: 12}, scratch=[flux],
    )
    u0, a0, u1, a1, u2, a2, u3, a3, k, rk, lam, grad, l3, send_o = result
    from_outer = lax.ppermute(send_o, both, outer)
    final, lam, l3, grad = call(
        lambda refs: fourth_kernel(geo, refs), "fourth",
        tuple(keep(x) for x in (u0, a0, u1, a1, u2, a2, u3, a3, rk, heat, from_inner, lam, l3, grad)), [VMEM] * 14,
        [plain(initial.shape), states[10], l3_shape, states[11]], out_specs=[HBM] + [VMEM] * 3,
        aliases={11: 1, 12: 2, 13: 3},
        scratch=[flux, pltpu.VMEM(initial.shape, F32), pltpu.SemaphoreType.DMA((top,))], mib=4,
    )
    part = (top, geo.rows // ways, geo.lanes)
    result = call(
        lambda refs: fifth_kernel(geo, ways, refs), "fifth",
        tuple(keep(x) for x in (u0, a0, u1, a1, rk, from_outer, lam, l3, grad)), [VMEM] * 9,
        [states[10], l3_shape, states[11]] + [pinned(part)] * ways, aliases={6: 0, 7: 1, 8: 2},
        scratch=[flux, pltpu.VMEM((geo.rows, geo.lanes), F32)],
    )
    parts = result[3:]
    arrived = [parts[0]]
    for way in range(1, ways):
        arrived.append(lax.ppermute(parts[way], "set", [(i, i ^ way) for i in range(ways)]))
    (owned,) = call(
        lambda refs: sum_kernel(geo, refs), "total", tuple(keep(x) for x in arrived), [VMEM] * ways, [plain(part)]
    )
    return (final, owned)


def solution(mesh):
    in_specs = (
        P("set", "space", None, None),
        P("space", None, None),
        P("set", "space", None, None),
        P("set"),
        P(),
        P(),
    )
    out_specs = (P("set", "space", None, None), P("space", "set", None))
    return jax.shard_map(local, mesh=mesh, in_specs=in_specs, out_specs=out_specs, check_vma=False)
```

time: 240 us -> 84 us (0.35)
  other arithmetic: 127 us -> 0 us
  Pallas kernels: 0 us -> 58 us
  starting transfers between devices: 56.6 us -> 12.2 us
  waiting for transfers between devices: 32.6 us -> 11.8 us
  between operations: 14.8 us -> 0.75 us
  local copies, waits for them, and re-layouts: 8.36 us -> 1.05 us
    add x8 -> x0, other arithmetic: 59.2 us -> none  [the longest x3 35.1 us: local(): adjoint = grad_temp + grad_coef * kappa * conduct_slope(centre_temp)]
    pallas_call x0 -> x7, Pallas kernels: none -> 58 us  [call(): pl.pallas_call(lambda *refs: body(refs), name=name, out_shape=tuple(outs)...]
    reduce_sum x5 -> x0, other arithmetic: 45.8 us -> none  [the longest x4 44.9 us: local(): gradient = gradient + jnp.sum(grad_coef * conduct(centre_temp), axis=0)]
    ppermute x18 -> x11, starting transfers between devices: 56.6 us -> 12.2 us  [the longest x3 5.74 us: local(): uo, ko, wo = (lax.ppermute(x, both, outer) for x in cuts[:3])]
    reduce_scatter x1 -> x0, waiting for transfers between devices: 22.6 us -> none  [local(): owned = lax.psum_scatter(gradient, 'set', scatter_dimension=1, tiled=True)]
    concatenate x8 -> x0, other arithmetic: 19.5 us -> none  [with_halo(): shard = jnp.concatenate([before, shard, after], axis=dim)]
    slice x9 -> x0, local copies, waits for them, and re-layouts: 5.48 us -> none  [the longest x4 3.24 us: with_halo(): initial = lax.slice_in_dim(shard, 0, width, axis=dim)]
    ppermute x18 -> x11, waiting for transfers between devices: 10 us -> 11.8 us  [the longest x3 11.6 us: local(): lax.ppermute(parts[way], 'set', [(i, i ^ way) for i in range(ways)])]
  transfers between devices with their start and end apart: 19 -> 11, of which waited for: 5 -> 3; matrix products, arithmetic and copies ran while one was open for 9% -> 0% of each run, Pallas kernels for 0% -> 59%
where the time goes in v1:
time: 84 us; the launch traced here: 83.8 us
  Pallas kernels  58 us (69%)
  starting transfers between devices  12.2 us (15%)
  waiting for transfers between devices  11.8 us (14%)
  local copies, waits for them, and re-layouts  1.05 us (1%)
    pallas_call x7, Pallas kernels, call(): pl.pallas_call(lambda *refs: body(refs), name=name, out_shape=tuple(outs)...  58 us
    ppermute x3, waiting for transfers between devices, local(): lax.ppermute(parts[way], 'set', [(i, i ^ way) for i in range(ways)])  11.6 us
    ppermute x3, starting transfers between devices, local(): uo, ko, wo = (lax.ppermute(x, both, outer) for x in cuts[:3])  5.74 us
    ppermute x3, starting transfers between devices, local(): lax.ppermute(parts[way], 'set', [(i, i ^ way) for i in range(ways)])  3.55 us
  transfers between devices with their start and end apart: 11, of which 3 were waited for; matrix products, arithmetic and copies ran while one was open for 0% of the time, Pallas kernels for 59%

profile of v1, /device:TPU:0, one launch (start us, length us, event | category | flops | bytes accessed | tf_op | source)
XLA Modules:
  0.0 83.8 jit_solution(3532949111489694539)
XLA Ops:
  0.6 0.0 copy-start.3
  0.6 0.0 copy-start.4
  0.7 0.0 copy-start.2
  0.7 4.5 %cut.1 = (f32[2,5,256,128]{3,2,1,0:T(8,128)}, f32[5,256,128]{2,1,0:T(8,128)}, f32[2,2,256,128]{3,2,1,0:T(8,128)}, f32[2,5,256,128]{3,2,1,0:T(8,128)}, f32[5,256,...) custom-call(f32[2,8,256,128]{3,2,1,0:T(8,128)} %refs_0_.3, f32[8,256,128]{2,1,0:T(8,128)} %refs_1_.3, f32[2,8,256,128]{3,2,1,0:T(8,128)} %refs_2_.3), custom_call_target="tpu_custom_call" | custom-call | tf_op jit(solution)/shard_map/cut/pallas_call | solution.py:476
  5.2 0.6 collective-permute-start.3
  5.8 2.6 %collective-permute-start = (f32[2,5,256,128]{3,2,1,0:T(8,128)}, f32[2,5,256,128]{3,2,1,0:T(8,128)}, u32[]{:S(2)}, u32[]{:S(2)}) collective-permute-start(f32[2,5,256,128]{3,2,1,0:T(8,128)} %get-tuple-element.57), channel_id=1, source_target_pairs={{4,8},{5,9},{6,10},{7,11},{8,4},{9,5},{10,6},{11,7},{12,16},{13,17... | collective-permute-start | bytes 3932168 | tf_op jit(solution)/shard_map/ppermute | solution.py:514
  8.3 0.2 collective-permute-start.5
  8.5 0.3 collective-permute-start.4
  8.8 1.2 %collective-permute-start.1 = (f32[5,256,128]{2,1,0:T(8,128)}, f32[5,256,128]{2,1,0:T(8,128)}, u32[]{:S(2)}, u32[]{:S(2)}) collective-permute-start(f32[5,256,128]{2,1,0:T(8,128)} %get-tuple-element.58), channel_id=1, source_target_pairs={{4,8},{5,9},{6,10},{7,11},{8,4},{9,5},{10,6},{11,7},{12,16},{13,17... | collective-permute-start | bytes 1966088 | tf_op jit(solution)/shard_map/ppermute | solution.py:514
  10.0 0.2 collective-permute-done.5.refs_2_
  10.2 0.0 copy-start
  10.2 0.8 %copy-done = f32[2,2,256,128]{3,2,1,0:T(8,128)} copy-done((f32[2,2,256,128]{3,2,1,0:T(8,128)}, f32[2,2,256,128]{3,2,1,0:T(8,128)S(1)}, u32[]{:S(2)}) %copy-start) | copy-done | bytes 524312
  11.1 2.0 %collective-permute-start.2 = (f32[2,2,256,128]{3,2,1,0:T(8,128)}, f32[2,2,256,128]{3,2,1,0:T(8,128)}, u32[]{:S(2)}, u32[]{:S(2)}) collective-permute-start(f32[2,2,256,128]{3,2,1,0:T(8,128)} %get-tuple-element.59), channel_id=1, source_target_pairs={{4,8},{5,9},{6,10},{7,11},{8,4},{9,5},{10,6},{11,7},{12,16},{13,17... | collective-permute-start | bytes 1572872 | tf_op jit(solution)/shard_map/ppermute | solution.py:514
  13.1 0.0 copy-done.3
  13.1 0.1 copy.40.refs_4_
  13.2 0.0 copy-done.4
  13.2 0.1 copy.41.refs_5_
  13.3 0.0 copy-done.2
  13.3 0.0 copy-start.1
  13.3 11.2 %first.1 = (f32[2,18,34,8,128]{4,3,2,1,0:T(8,128)S(1)}, f32[2,18,34,8,128]{4,3,2,1,0:T(8,128)S(1)}, f32[2,16,34,8,128]{4,3,2,1,0:T(8,128)S(1)}, f32[2,16,34,8,12...) custom-call(f32[2,8,256,128]{3,2,1,0:T(8,128)} %refs_0_.3, ...), custom_call_target="tpu_custom_call" | custom-call | tf_op jit(solution)/shard_map/first/pallas_call | solution.py:476
  24.5 0.0 collective-permute-done.4.refs_1_
  24.5 0.0 collective-permute-done.3.refs_0_
  24.5 0.0 copy-done.1
  24.5 13.9 %second.1 = (f32[2,18,34,8,128]{4,3,2,1,0:T(8,128)S(1)}, f32[2,18,34,8,128]{4,3,2,1,0:T(8,128)S(1)}, f32[2,16,34,8,128]{4,3,2,1,0:T(8,128)S(1)}, f32[2,16,34,8,1...) custom-call(f32[2,5,256,128]{3,2,1,0:T(8,128)} %collective-permute-d, ...), custom_call_target="tpu_custom_call", output_to_operand_aliasing={{0}: (3, {}), {1}: (4, {}), {2}: (5, {}), {3}: (6, {}), {4}... | custom-call | tf_op jit(solution)/shard_map/second/pallas_call | solution.py:476
  38.4 0.3 collective-permute-start.6
  38.7 0.0 collective-permute-done.2.refs_2_
  38.7 0.0 collective-permute-done.1.refs_1_
  38.7 0.0 collective-permute-done.refs_0_
  38.7 11.5 %third.1 = (f32[2,18,34,8,128]{4,3,2,1,0:T(8,128)S(1)}, f32[2,18,34,8,128]{4,3,2,1,0:T(8,128)S(1)}, f32[2,16,34,8,128]{4,3,2,1,0:T(8,128)S(1)}, f32[2,16,34,8,12...) custom-call(f32[2,5,256,128]{3,2,1,0:T(8,128)} %collective-permute-d, ...), custom_call_target="tpu_custom_call", output_to_operand_aliasing={{0}: (3, {}), {1}: (4, {}), {2}: (5, {}), {3}: (6, {}), {4}... | custom-call | tf_op jit(solution)/shard_map/third/pallas_call | solution.py:476
  50.3 1.6 %collective-permute-start.7 = (f32[2,2,34,8,128]{4,3,2,1,0:T(8,128)S(1)}, f32[2,2,34,8,128]{4,3,2,1,0:T(8,128)S(1)}, u32[]{:S(2)}, u32[]{:S(2)}) collective-permute-start(f32[2,2,34,8,128]{4,3,2,1,0:T(8,128)S(1)} %get-tuple-element.104), channel_id=1, source_target_pairs={{4,8},{5,9},{6,10},{7,11},{8,4},{9,5},{10,6},{11,7},{12,16},{13,17... | collective-permute-start | bytes 1671176 | tf_op jit(solution)/shard_map/ppermute | solution.py:545
  51.8 0.0 collective-permute-done.6.refs_10_
  51.8 13.1 %fourth.1 = (f32[2,8,256,128]{3,2,1,0:T(8,128)}, f32[2,12,34,8,128]{4,3,2,1,0:T(8,128)S(1)}, f32[2,10,34,8,128]{4,3,2,1,0:T(8,128)S(1)}, f32[10,32,8,128]{3,2,1,0:T(8,128)S(1)}) custom-call(f32[2,18,34,8,128]{4,3,2,1,0:T(8,128)S(1)} %get-tuple-element.90.refs_0_, ...), custom_call_target="tpu_custom_call", output_to_operand_aliasing={{1}: (11, {}), {2}: (12, {}), {3}: (13, {})} | custom-call | tf_op jit(solution)/shard_map/fourth/pallas_call | solution.py:476
  65.0 0.0 collective-permute-done.7.refs_5_
  65.0 2.8 %fifth.1 = (f32[2,12,34,8,128]{4,3,2,1,0:T(8,128)S(1)}, f32[2,10,34,8,128]{4,3,2,1,0:T(8,128)S(1)}, f32[10,32,8,128]{3,2,1,0:T(8,128)S(1)}, f32[8,64,128]{2,1,0:...) custom-call(f32[2,18,34,8,128]{4,3,2,1,0:T(8,128)S(1)} %get-tuple-el, ...), custom_call_target="tpu_custom_call", output_to_operand_aliasing={{0}: (6, {}), {1}: (7, {}), {2}: (8, {})} | custom-call | tf_op jit(solution)/shard_map/fifth/pallas_call | solution.py:476
  67.8 0.6 collective-permute-start.8
  68.4 1.5 %collective-permute-start.9 = (f32[8,64,128]{2,1,0:T(8,128)S(1)}, f32[8,64,128]{2,1,0:T(8,128)S(1)}, u32[]{:S(2)}, u32[]{:S(2)}) collective-permute-start(f32[8,64,128]{2,1,0:T(8,128)S(1)} %get-tuple-element.110), channel_id=1, source_target_pairs={{0,2},{1,3},{2,0},{3,1},{4,6},{5,7},{6,4},{7,5},{8,10},{9,11},{10,... | collective-permute-start | bytes 786440 | tf_op jit(solution)/shard_map/ppermute | solution.py:563
  70.0 1.4 %collective-permute-start.10 = (f32[8,64,128]{2,1,0:T(8,128)S(1)}, f32[8,64,128]{2,1,0:T(8,128)S(1)}, u32[]{:S(2)}, u32[]{:S(2)}) collective-permute-start(f32[8,64,128]{2,1,0:T(8,128)S(1)} %get-tuple-element.111), channel_id=1, source_target_pairs={{0,3},{1,2},{2,1},{3,0},{4,7},{5,6},{6,5},{7,4},{8,11},{9,10},{10,... | collective-permute-start | bytes 786440 | tf_op jit(solution)/shard_map/ppermute | solution.py:563
  71.4 5.0 %collective-permute-done.8.refs_1_ = f32[8,64,128]{2,1,0:T(8,128)S(1)} collective-permute-done((f32[8,64,128]{2,1,0:T(8,128)S(1)}, f32[8,64,128]{2,1,0:T(8,128)S(1)}, u32[]{:S(2)}, u32[]{:S(2)}) %collective-permute-start.8) | collective-permute-done | bytes 262176 | tf_op jit(solution)/shard_map/ppermute | solution.py:563
  76.4 0.0 collective-permute-done.9.refs_2_
  76.4 6.6 %collective-permute-done.10.refs_3_ = f32[8,64,128]{2,1,0:T(8,128)S(1)} collective-permute-done((f32[8,64,128]{2,1,0:T(8,128)S(1)}, f32[8,64,128]{2,1,0:T(8,128)S(1)}, u32[]{:S(2)}, u32[]{:S(2)}) %collective-permute-start.10) | collective-permute-done | bytes 262176 | tf_op jit(solution)/shard_map/ppermute | solution.py:563
  83.0 0.8 total.1
Async XLA Ops:
  0.6 12.5 %copy-start.3 = (s32[64,4]{0,1:T(4,128)S(1)}, s32[64,4]{0,1:T(4,128)}, u32[]{:S(2)}) copy-start(s32[64,4]{0,1:T(4,128)} %param.10) | copy-start | bytes 3076
  0.6 12.5 %copy-start.4 = (s32[64,4]{0,1:T(4,128)S(1)}, s32[64,4]{0,1:T(4,128)}, u32[]{:S(2)}) copy-start(s32[64,4]{0,1:T(4,128)} %param.11) | copy-start | bytes 3076
  0.7 12.6 %copy-start.2 = (s32[2]{0:T(128)S(1)}, s32[2]{0:T(128)}, u32[]{:S(2)}) copy-start(s32[2]{0:T(128)} %refs_3_.1) | copy-start | bytes 28
  5.2 19.3 %collective-permute-start.3 = (f32[2,5,256,128]{3,2,1,0:T(8,128)}, f32[2,5,256,128]{3,2,1,0:T(8,128)}, u32[]{:S(2)}, u32[]{:S(2)}) collective-permute-start(f32[2,5,256,128]{3,2,1,0:T(8,128)} %get-tuple-element.60), channel_id=1, source_target_pairs={{0,4},{4,0},{8,12},{12,8},{16,20},{20,16},{24,28},{28,24},{1,5},{5... | collective-permute-start | bytes 3932168 | tf_op jit(solution)/shard_map/ppermute | solution.py:515
  5.8 32.9 %collective-permute-start = (f32[2,5,256,128]{3,2,1,0:T(8,128)}, f32[2,5,256,128]{3,2,1,0:T(8,128)}, u32[]{:S(2)}, u32[]{:S(2)}) collective-permute-start(f32[2,5,256,128]{3,2,1,0:T(8,128)} %get-tuple-element.57), channel_id=1, source_target_pairs={{4,8},{5,9},{6,10},{7,11},{8,4},{9,5},{10,6},{11,7},{12,16},{13,17... | collective-permute-start | bytes 3932168 | tf_op jit(solution)/shard_map/ppermute | solution.py:514
  8.3 1.9 %collective-permute-start.5 = (f32[2,2,256,128]{3,2,1,0:T(8,128)S(1)}, f32[2,2,256,128]{3,2,1,0:T(8,128)S(1)}, u32[]{:S(2)}, u32[]{:S(2)}) collective-permute-start(f32[2,2,256,128]{3,2,1,0:T(8,128)S(1)} %get-tuple-element.62), channel_id=1, source_target_pairs={{0,4},{4,0},{8,12},{12,8},{16,20},{20,16},{24,28},{28,24},{1,5},{5... | collective-permute-start | bytes 1572872 | tf_op jit(solution)/shard_map/ppermute | solution.py:515
  8.5 15.9 %collective-permute-start.4 = (f32[5,256,128]{2,1,0:T(8,128)}, f32[5,256,128]{2,1,0:T(8,128)}, u32[]{:S(2)}, u32[]{:S(2)}) collective-permute-start(f32[5,256,128]{2,1,0:T(8,128)} %get-tuple-element.61), channel_id=1, source_target_pairs={{0,4},{4,0},{8,12},{12,8},{16,20},{20,16},{24,28},{28,24},{1,5},{5... | collective-permute-start | bytes 1966088 | tf_op jit(solution)/shard_map/ppermute | solution.py:515
  8.8 29.9 %collective-permute-start.1 = (f32[5,256,128]{2,1,0:T(8,128)}, f32[5,256,128]{2,1,0:T(8,128)}, u32[]{:S(2)}, u32[]{:S(2)}) collective-permute-start(f32[5,256,128]{2,1,0:T(8,128)} %get-tuple-element.58), channel_id=1, source_target_pairs={{4,8},{5,9},{6,10},{7,11},{8,4},{9,5},{10,6},{11,7},{12,16},{13,17... | collective-permute-start | bytes 1966088 | tf_op jit(solution)/shard_map/ppermute | solution.py:514
  10.2 0.8 %copy-start = (f32[2,2,256,128]{3,2,1,0:T(8,128)}, f32[2,2,256,128]{3,2,1,0:T(8,128)S(1)}, u32[]{:S(2)}) copy-start(f32[2,2,256,128]{3,2,1,0:T(8,128)S(1)} %collective-permute-done.5.refs_2_) | copy-start | bytes 1572868
  11.1 27.6 %collective-permute-start.2 = (f32[2,2,256,128]{3,2,1,0:T(8,128)}, f32[2,2,256,128]{3,2,1,0:T(8,128)}, u32[]{:S(2)}, u32[]{:S(2)}) collective-permute-start(f32[2,2,256,128]{3,2,1,0:T(8,128)} %get-tuple-element.59), channel_id=1, source_target_pairs={{4,8},{5,9},{6,10},{7,11},{8,4},{9,5},{10,6},{11,7},{12,16},{13,17... | collective-permute-start | bytes 1572872 | tf_op jit(solution)/shard_map/ppermute | solution.py:514
  13.3 11.2 %copy-start.1 = (f32[2,2,256,128]{3,2,1,0:T(8,128)S(1)}, f32[2,2,256,128]{3,2,1,0:T(8,128)}, u32[]{:S(2)}) copy-start(f32[2,2,256,128]{3,2,1,0:T(8,128)} %copy-done) | copy-start | bytes 1572868
  38.4 13.4 %collective-permute-start.6 = (f32[2,2,34,8,128]{4,3,2,1,0:T(8,128)S(1)}, f32[2,2,34,8,128]{4,3,2,1,0:T(8,128)S(1)}, u32[]{:S(2)}, u32[]{:S(2)}) collective-permute-start(f32[2,2,34,8,128]{4,3,2,1,0:T(8,128)S(1)} %get-tuple-element.99), channel_id=1, source_target_pairs={{0,4},{4,0},{8,12},{12,8},{16,20},{20,16},{24,28},{28,24},{1,5},{5... | collective-permute-start | bytes 1671176 | tf_op jit(solution)/shard_map/ppermute | solution.py:538
  50.3 14.7 %collective-permute-start.7 = (f32[2,2,34,8,128]{4,3,2,1,0:T(8,128)S(1)}, f32[2,2,34,8,128]{4,3,2,1,0:T(8,128)S(1)}, u32[]{:S(2)}, u32[]{:S(2)}) collective-permute-start(f32[2,2,34,8,128]{4,3,2,1,0:T(8,128)S(1)} %get-tuple-element.104), channel_id=1, source_target_pairs={{4,8},{5,9},{6,10},{7,11},{8,4},{9,5},{10,6},{11,7},{12,16},{13,17... | collective-permute-start | bytes 1671176 | tf_op jit(solution)/shard_map/ppermute | solution.py:545
  67.8 8.6 %collective-permute-start.8 = (f32[8,64,128]{2,1,0:T(8,128)S(1)}, f32[8,64,128]{2,1,0:T(8,128)S(1)}, u32[]{:S(2)}, u32[]{:S(2)}) collective-permute-start(f32[8,64,128]{2,1,0:T(8,128)S(1)} %get-tuple-element.109), channel_id=1, source_target_pairs={{0,1},{1,0},{2,3},{3,2},{4,5},{5,4},{6,7},{7,6},{8,9},{9,8},{10,11... | collective-permute-start | bytes 786440 | tf_op jit(solution)/shard_map/ppermute | solution.py:563
  68.4 8.0 %collective-permute-start.9 = (f32[8,64,128]{2,1,0:T(8,128)S(1)}, f32[8,64,128]{2,1,0:T(8,128)S(1)}, u32[]{:S(2)}, u32[]{:S(2)}) collective-permute-start(f32[8,64,128]{2,1,0:T(8,128)S(1)} %get-tuple-element.110), channel_id=1, source_target_pairs={{0,2},{1,3},{2,0},{3,1},{4,6},{5,7},{6,4},{7,5},{8,10},{9,11},{10,... | collective-permute-start | bytes 786440 | tf_op jit(solution)/shard_map/ppermute | solution.py:563
  70.0 13.0 %collective-permute-start.10 = (f32[8,64,128]{2,1,0:T(8,128)S(1)}, f32[8,64,128]{2,1,0:T(8,128)S(1)}, u32[]{:S(2)}, u32[]{:S(2)}) collective-permute-start(f32[8,64,128]{2,1,0:T(8,128)S(1)} %get-tuple-element.111), channel_id=1, source_target_pairs={{0,3},{1,2},{2,1},{3,0},{4,7},{5,6},{6,5},{7,4},{8,11},{9,10},{10,... | collective-permute-start | bytes 786440 | tf_op jit(solution)/shard_map/ppermute | solution.py:563
